TPU v7x, 32 devices: a whole 2x2x4 slice. The times are simulated.
32 devices in a mesh: dp: 16 (over z, y, core), seq: 2 (over x).
Axes of the slice: x: 2, y: 2, z: 4, core: 2. Of those that a mesh axis runs over, the one named last changes fastest.
Arguments:
- clip_tokens: bfloat16 [16, 1024, 1024], P('dp', 'seq'), may hold values from -6 to 6
- adapter_index: int32 [16], P('dp'), may hold values from 0 to 7
- ln1_gain: float32 [1024], replicated, may hold values from 0.25 to 1.75
- ln1_bias: float32 [1024], replicated, may hold values from -1.8 to 1.8
- qkv_weight: bfloat16 [1024, 3072], replicated, may hold values from -0.1875 to 0.1875
- qkv_bias: float32 [3072], replicated, may hold values from -1.8 to 1.8
- qkv_down: bfloat16 [8, 16, 1024], replicated, may hold values from -0.1875 to 0.1875
- qkv_up: bfloat16 [8, 16, 3072], replicated, may hold values from -1.5 to 1.5
- out_weight: bfloat16 [1024, 1024], replicated, may hold values from -3 to 3
- out_bias: float32 [1024], replicated, may hold values from -1.8 to 1.8
- out_down: bfloat16 [8, 16, 1024], replicated, may hold values from -3 to 3
- out_up: bfloat16 [8, 16, 1024], replicated, may hold values from -1.5 to 1.5
- ln2_gain: float32 [1024], replicated, may hold values from 0.25 to 1.75
- ln2_bias: float32 [1024], replicated, may hold values from -1.8 to 1.8
- fc1_weight: bfloat16 [1024, 4096], replicated, may hold values from -0.1875 to 0.1875
- fc1_bias: float32 [4096], replicated, may hold values from -1.8 to 1.8
- fc1_down: bfloat16 [8, 16, 1024], replicated, may hold values from -0.1875 to 0.1875
- fc1_up: bfloat16 [8, 16, 4096], replicated, may hold values from -1.5 to 1.5
- fc2_weight: bfloat16 [4096, 1024], replicated, may hold values from -0.09375 to 0.09375
- fc2_bias: float32 [1024], replicated, may hold values from -1.8 to 1.8
- fc2_down: bfloat16 [8, 16, 4096], replicated, may hold values from -0.09375 to 0.09375
- fc2_up: bfloat16 [8, 16, 1024], replicated, may hold values from -1.5 to 1.5
- cotangent: bfloat16 [16, 1024, 1024], P('dp', 'seq'), may hold values from -6 to 6
Outputs:
- block_output: bfloat16 [16, 1024, 1024], P('dp', 'seq')
- input_grad: float32 [16, 1024, 1024], P('dp', 'seq')
- grad_qkv_down: float32 [8, 16, 1024], replicated
- grad_qkv_up: float32 [8, 16, 3072], replicated
- grad_out_down: float32 [8, 16, 1024], replicated
- grad_out_up: float32 [8, 16, 1024], replicated
- grad_fc1_down: float32 [8, 16, 1024], replicated
- grad_fc1_up: float32 [8, 16, 4096], replicated
- grad_fc2_down: float32 [8, 16, 4096], replicated
- grad_fc2_up: float32 [8, 16, 1024], replicated
All inputs are finite; a program needn't handle non-finite values.
Results may differ from a plain program's by a relative error of at most 0.023.
Values may be sent and summed in bfloat16 or wider, within the bound.
No kernel may reach another device: no remote copies, remote signals or barrier semaphores. Data moves between devices by JAX's collectives and lax.ppermute only.
A program may use at most 192 MiB of HBM per device.

v0:
```python
import jax
import jax.numpy as jnp
from jax import lax
from jax.sharding import PartitionSpec as P

HEADS = 16
HD = 64
FF = 4096
NADAPT = 8
GRID = 16
EPSILON = 1e-06
span_keys = 512


def norm_rows(values, gain, shift):
    centre = values - jnp.mean(values, axis=-1, keepdims=True)
    spread = lax.rsqrt(jnp.mean(centre * centre, axis=-1, keepdims=True) + EPSILON)
    normed = centre * spread
    return (normed * gain + shift, normed, spread)


def norm_back(grad_rows, normed, spread, gain):
    scaled = grad_rows * gain
    first_mean = jnp.mean(scaled, axis=-1, keepdims=True)
    second_mean = jnp.mean(scaled * normed, axis=-1, keepdims=True)
    return spread * (scaled - first_mean - normed * second_mean)


def rotary_tables(first_token, count_rows, head_size, grid_side):
    half_size = head_size // 2
    side_pairs = half_size // 3
    lead_pairs = half_size - 2 * side_pairs
    token_index = first_token + jnp.arange(count_rows, dtype=jnp.int32)
    frame = token_index // (grid_side * grid_side)
    row_pos = token_index // grid_side % grid_side
    col_pos = token_index % grid_side
    pair_index = jnp.arange(half_size, dtype=jnp.int32)
    axis_pick = jnp.where(
        pair_index < lead_pairs, 0, jnp.where(pair_index < lead_pairs + side_pairs, 1, 2)
    )
    local_pair = jnp.where(
        axis_pick == 0,
        pair_index,
        jnp.where(axis_pick == 1, pair_index - lead_pairs, pair_index - lead_pairs - side_pairs),
    )
    total_pairs = jnp.where(axis_pick == 0, lead_pairs, side_pairs)
    frequency = jnp.power(
        10000.0, -local_pair.astype(jnp.float32) / total_pairs.astype(jnp.float32)
    )
    position = jnp.where(
        axis_pick[None, :] == 0,
        frame[:, None],
        jnp.where(axis_pick[None, :] == 1, row_pos[:, None], col_pos[:, None]),
    ).astype(jnp.float32)
    angles = position * frequency[None, :]
    return (jnp.cos(angles), jnp.sin(angles))


def rotate(values, cosine, sine):
    half_size = values.shape[-1] // 2
    first_half = values[..., :half_size]
    second_half = values[..., half_size:]
    cos_rows = cosine[:, None, :]
    sin_rows = sine[:, None, :]
    return jnp.concatenate(
        [
            first_half * cos_rows - second_half * sin_rows,
            first_half * sin_rows + second_half * cos_rows,
        ],
        axis=-1,
    )


def unrotate(values, cosine, sine):
    half_size = values.shape[-1] // 2
    first_half = values[..., :half_size]
    second_half = values[..., half_size:]
    cos_rows = cosine[:, None, :]
    sin_rows = sine[:, None, :]
    return jnp.concatenate(
        [
            first_half * cos_rows + second_half * sin_rows,
            second_half * cos_rows - first_half * sin_rows,
        ],
        axis=-1,
    )


def project(inputs, weight, bias_row, down_pick, up_pick):
    low_rank = jnp.einsum(
        "crd,cad->cra", inputs, down_pick, preferred_element_type=jnp.float32
    ).astype(jnp.bfloat16)
    main_part = jnp.einsum("crd,de->cre", inputs, weight, preferred_element_type=jnp.float32)
    side_part = jnp.einsum("cra,cae->cre", low_rank, up_pick, preferred_element_type=jnp.float32)
    return (main_part + bias_row + side_part, low_rank)


def project_back(grad_low, inputs, low_rank, weight, down_pick, up_pick):
    main_part = jnp.einsum("cre,de->crd", grad_low, weight, preferred_element_type=jnp.float32)
    rank_grad = jnp.einsum(
        "cre,cae->cra", grad_low, up_pick, preferred_element_type=jnp.float32
    ).astype(jnp.bfloat16)
    backward = main_part + jnp.einsum(
        "cra,cad->crd", rank_grad, down_pick, preferred_element_type=jnp.float32
    )
    grad_up = jnp.einsum("cra,cre->cae", low_rank, grad_low, preferred_element_type=jnp.float32)
    grad_down = jnp.einsum("cra,crd->cad", rank_grad, inputs, preferred_element_type=jnp.float32)
    return (backward, grad_down, grad_up)


def over_blocks(block_step, carried, key_rows, value_rows, first_row):
    key_count = key_rows.shape[1]
    block_size = min(key_count, span_keys)
    full_blocks = key_count // block_size

    def one_block(number, inner):
        offset = number * block_size
        return block_step(
            inner,
            lax.dynamic_slice_in_dim(key_rows, offset, block_size, 1),
            lax.dynamic_slice_in_dim(value_rows, offset, block_size, 1),
            first_row + offset,
        )

    carried = lax.fori_loop(0, full_blocks, one_block, carried)
    return carried


def body(
    clip_tokens,
    adapter_index,
    ln1_gain,
    ln1_bias,
    qkv_weight,
    qkv_bias,
    qkv_down,
    qkv_up,
    out_weight,
    out_bias,
    out_down,
    out_up,
    ln2_gain,
    ln2_bias,
    fc1_weight,
    fc1_bias,
    fc1_down,
    fc1_up,
    fc2_weight,
    fc2_bias,
    fc2_down,
    fc2_up,
    cotangent,
):
    clip_count, row_count, model_width = clip_tokens.shape
    score_scale = HD ** (-0.5)
    head_shape = (clip_count, row_count, HEADS, HD)
    onehot = (adapter_index[:, None] == jnp.arange(NADAPT, dtype=jnp.int32)[None, :]).astype(
        jnp.bfloat16
    )

    def select(table_rows):
        return jnp.einsum(
            "ca,ard->crd", onehot, table_rows, preferred_element_type=jnp.float32
        ).astype(jnp.bfloat16)

    picks = [
        select(table_rows)
        for table_rows in (qkv_down, qkv_up, out_down, out_up, fc1_down, fc1_up, fc2_down, fc2_up)
    ]
    inputs = clip_tokens.astype(jnp.float32)
    first_norm, first_normed, first_spread = norm_rows(inputs, ln1_gain, ln1_bias)
    first_in = first_norm.astype(jnp.bfloat16)
    qkv_pre, rank_qkv = project(first_in, qkv_weight, qkv_bias, picks[0], picks[1])
    cosine, sine = rotary_tables(lax.axis_index("seq") * row_count, row_count, HD, GRID)
    query_heads = rotate(qkv_pre[..., :model_width].reshape(head_shape), cosine, sine).astype(
        jnp.bfloat16
    )
    key_low = (
        rotate(qkv_pre[..., model_width : 2 * model_width].reshape(head_shape), cosine, sine)
        .astype(jnp.bfloat16)
        .reshape(clip_count, row_count, model_width)
    )
    value_low = qkv_pre[..., 2 * model_width :].astype(jnp.bfloat16)

    def forward_step(carried, key_rows, value_rows, offset):
        row_max, row_sum, weighted = carried
        key_heads = key_rows.reshape(clip_count, key_rows.shape[1], HEADS, HD)
        value_heads = value_rows.reshape(clip_count, value_rows.shape[1], HEADS, HD)
        scores = (
            jnp.einsum(
                "cqhd,ckhd->chqk", query_heads, key_heads, preferred_element_type=jnp.float32
            )
            * score_scale
        )
        new_max = jnp.maximum(row_max, jnp.max(scores, axis=-1))
        weights = jnp.exp(scores - new_max[..., None])
        factor = jnp.exp(row_max - new_max)
        row_sum = row_sum * factor + jnp.sum(weights, axis=-1)
        update = jnp.einsum(
            "chqk,ckhd->cqhd",
            weights.astype(jnp.bfloat16),
            value_heads,
            preferred_element_type=jnp.float32,
        )
        weighted = weighted * jnp.transpose(factor, (0, 2, 1))[..., None] + update
        return (new_max, row_sum, weighted)

    init_state = (
        jnp.full((clip_count, HEADS, row_count), -1e30, jnp.float32),
        jnp.zeros((clip_count, HEADS, row_count), jnp.float32),
        jnp.zeros(head_shape, jnp.float32),
    )
    key_all, value_all = (
        lax.all_gather(key_low, "seq", axis=1, tiled=True),
        lax.all_gather(value_low, "seq", axis=1, tiled=True),
    )
    row_max, row_sum, weighted = over_blocks(forward_step, init_state, key_all, value_all, 0)
    out_heads = weighted / jnp.transpose(row_sum, (0, 2, 1))[..., None]
    log_total = row_max + jnp.log(row_sum)
    mixed_low = out_heads.reshape(clip_count, row_count, model_width).astype(jnp.bfloat16)
    attn_pre, rank_out = project(mixed_low, out_weight, out_bias, picks[2], picks[3])
    middle = inputs + attn_pre
    second_norm, second_normed, second_spread = norm_rows(middle, ln2_gain, ln2_bias)
    second_in = second_norm.astype(jnp.bfloat16)
    hidden, rank_fc1 = project(second_in, fc1_weight, fc1_bias, picks[4], picks[5])

    def exact_gelu(values):
        return jax.nn.gelu(values, approximate=False)

    active, gelu_back = jax.vjp(exact_gelu, hidden)
    active_low = active.astype(jnp.bfloat16)
    fc2_pre, rank_fc2 = project(active_low, fc2_weight, fc2_bias, picks[6], picks[7])
    block_output = (middle + fc2_pre).astype(jnp.bfloat16)
    grad_active, down_fc2, up_fc2 = project_back(
        cotangent, active_low, rank_fc2, fc2_weight, picks[6], picks[7]
    )
    grad_hidden = gelu_back(grad_active)[0].astype(jnp.bfloat16)
    grad_second, down_fc1, up_fc1 = project_back(
        grad_hidden, second_in, rank_fc1, fc1_weight, picks[4], picks[5]
    )
    grad_middle = cotangent.astype(jnp.float32) + norm_back(
        grad_second, second_normed, second_spread, ln2_gain
    )
    grad_mixed, down_out, up_out = project_back(
        grad_middle.astype(jnp.bfloat16), mixed_low, rank_out, out_weight, picks[2], picks[3]
    )
    grad_heads = grad_mixed.astype(jnp.bfloat16).reshape(head_shape)
    row_delta = jnp.transpose(
        jnp.sum(grad_heads.astype(jnp.float32) * out_heads, axis=-1), (0, 2, 1)
    )

    def score_block(query_rows, grad_rows, log_rows, delta_rows, key_heads, value_heads):
        scores = (
            jnp.einsum("cqhd,ckhd->chqk", query_rows, key_heads, preferred_element_type=jnp.float32)
            * score_scale
        )
        attn_prob = jnp.exp(scores - log_rows[..., None])
        grad_prob = jnp.einsum(
            "cqhd,ckhd->chqk", grad_rows, value_heads, preferred_element_type=jnp.float32
        )
        grad_score = (attn_prob * (grad_prob - delta_rows[..., None])).astype(jnp.bfloat16)
        return (attn_prob, grad_score)

    def backward_step(carried, key_rows, value_rows, offset):
        grad_query, key_full, value_full = carried
        key_heads = key_rows.reshape(clip_count, key_rows.shape[1], HEADS, HD)
        value_heads = value_rows.reshape(clip_count, value_rows.shape[1], HEADS, HD)
        attn_prob, grad_score = score_block(
            query_heads, grad_heads, log_total, row_delta, key_heads, value_heads
        )
        grad_query = (
            grad_query
            + jnp.einsum(
                "chqk,ckhd->cqhd", grad_score, key_heads, preferred_element_type=jnp.float32
            )
            * score_scale
        )
        key_part = (
            jnp.einsum(
                "chqk,cqhd->ckhd", grad_score, query_heads, preferred_element_type=jnp.float32
            )
            * score_scale
        )
        value_part = jnp.einsum(
            "chqk,cqhd->ckhd",
            attn_prob.astype(jnp.bfloat16),
            grad_heads,
            preferred_element_type=jnp.float32,
        )
        key_full = lax.dynamic_update_slice_in_dim(
            key_full, key_part.reshape(clip_count, key_rows.shape[1], model_width), offset, 1
        )
        value_full = lax.dynamic_update_slice_in_dim(
            value_full, value_part.reshape(clip_count, key_rows.shape[1], model_width), offset, 1
        )
        return (grad_query, key_full, value_full)

    whole_rows = row_count * lax.axis_size("seq")
    back_init = (
        jnp.zeros(head_shape, jnp.float32),
        jnp.zeros((clip_count, whole_rows, model_width), jnp.float32),
        jnp.zeros((clip_count, whole_rows, model_width), jnp.float32),
    )
    back_result = over_blocks(backward_step, back_init, key_all, value_all, 0)
    grad_query, key_full, value_full = back_result
    key_grad, value_grad = (
        lax.psum_scatter(
            key_full.astype(jnp.bfloat16), "seq", scatter_dimension=1, tiled=True
        ).astype(jnp.float32),
        lax.psum_scatter(
            value_full.astype(jnp.bfloat16), "seq", scatter_dimension=1, tiled=True
        ).astype(jnp.float32),
    )
    grad_qkv = jnp.concatenate(
        [
            unrotate(grad_query, cosine, sine).reshape(clip_count, row_count, model_width),
            unrotate(key_grad.reshape(head_shape), cosine, sine).reshape(
                clip_count, row_count, model_width
            ),
            value_grad,
        ],
        axis=-1,
    ).astype(jnp.bfloat16)
    grad_first, down_qkv, up_qkv = project_back(
        grad_qkv, first_in, rank_qkv, qkv_weight, picks[0], picks[1]
    )
    input_grad = grad_middle + norm_back(grad_first, first_normed, first_spread, ln1_gain)
    packed_clip = jnp.concatenate(
        [down_qkv, up_qkv, down_out, up_out, down_fc1, up_fc1, down_fc2, up_fc2], axis=2
    )
    packed = jnp.einsum(
        "ca,crw->arw", onehot.astype(jnp.float32), packed_clip, precision=lax.Precision.HIGHEST
    )
    summed = lax.psum(packed.astype(jnp.bfloat16), "dp")
    owned = lax.psum_scatter(summed, "seq", scatter_dimension=2, tiled=True).astype(jnp.float32)
    gathered = lax.all_gather(owned.astype(jnp.bfloat16), "seq", axis=2, tiled=True).astype(
        owned.dtype
    )
    widths = [
        model_width,
        3 * model_width,
        model_width,
        model_width,
        model_width,
        FF,
        FF,
        model_width,
    ]
    results = []
    position = 0
    for span_width in widths:
        results.append(gathered[:, :, position : position + span_width])
        position = position + span_width
    return (
        block_output,
        input_grad,
        results[0],
        results[1],
        results[2],
        results[3],
        results[4],
        results[5],
        results[6],
        results[7],
    )


def solution(mesh):
    return jax.shard_map(
        body,
        mesh=mesh,
        in_specs=(
            P("dp", "seq", None),
            P("dp"),
            P(),
            P(),
            P(),
            P(),
            P(),
            P(),
            P(),
            P(),
            P(),
            P(),
            P(),
            P(),
            P(),
            P(),
            P(),
            P(),
            P(),
            P(),
            P(),
            P(),
            P("dp", "seq", None),
        ),
        out_specs=(
            P("dp", "seq", None),
            P("dp", "seq", None),
            P(),
            P(),
            P(),
            P(),
            P(),
            P(),
            P(),
            P(),
        ),
        check_vma=False,
    )
```

profile of v0, /device:TPU:0, one launch (start us, length us, event | category | flops | bytes accessed | tf_op | source)
XLA Modules:
  0.0 613.7 jit_solution(2214221213722635700)
XLA Ops:
  12.4 6.8 %fusion.113 = f32[512,3072]{1,0:T(8,128)S(1)} fusion(bf16[1024,3072]{1,0:T(8,128)(2,1)} %param.31, bf16[1,512,1024]{2,1,0:T(8,128)(2,1)} %param.27, f32[1024]{0:T(1024)} %param.30, f32[1024]{0:T(1024)} %param.29, f32[512]{0:T(512)S(1)} %add_rsqrt_fusion.1, f32[512]{0:T(512)S(1)} %broadcast_multiply_fusion.5), kind=kOutput, calls=%fused_computation.224 | convolution fusion | flops 3224371200 | bytes 13643776 | tf_op jit(solution)/shard_map/crd,de->cre/dot_general | solution.py:93
  25.5 4.8 fusion.116
  55.9 10.4 %fusion.62 = f32[512,4096]{1,0:T(8,128)} fusion(bf16[4096,1024]{1,0:T(8,128)(2,1)} %param.45, bf16[1,512,1024]{2,1,0:T(8,128)(2,1)S(1)} %copy-done.23), kind=kOutput, calls=%fused_computation.125 | convolution fusion | flops 4294967296 | bytes 17825792 | tf_op jit(solution)/shard_map/cre,de->crd/dot_general | solution.py:99
  70.2 26.5 %all-gather.4.cloned.1.call-done = bf16[1,1024,1024]{1,2,0:T(8,128)(2,1)} async-done(((bf16[1,512,1024]{1,2,0:T(8,128)(2,1)}), bf16[1,1024,1024]{1,2,0:T(8,128)(2,1)}) %all-gather.4.cloned.1.call-update) | async-done | bytes 2097168 | tf_op jit(solution)/shard_map/all_gather | solution.py:214
  96.6 60.7 %while.36 = (s32[]{:T(128)}, f32[1,16,512]{2,1,0:T(8,128)S(1)}, f32[1,16,512]{2,1,0:T(8,128)S(1)}, f32[1,512,16,64]{1,3,2,0:T(8,128)}, bf16[1,1024,1024]{1,2,0:T...) while((s32[]{:T(128)}, f32[1,16,512]{2,1,0:T(8,128)S(1)}, ...), condition=%wide.region_5.6_spmd.clone, body=%wide.region_2.5_spmd.clone.sunk | while | flops 1108918272 | bytes 66584780 | solution.py:125
  99.3 8.2 %bitcast_reduce_fusion.2 = (f32[16,512]{1,0:T(8,128)S(1)}, f32[16,512,512]{2,1,0:T(8,128)}) fusion(bf16[512,16,64]{0,2,1:T(8,128)(2,1)S(1)} %bitcast.339, bf16[1,512,16,64]{1,3,2,0:T(8,128)(2,1)S(1)} %get-tuple-element.629), kind=kOutput, calls=%fused_computation.1.clone.1 | convolution fusion | flops 545251328 | bytes 18907136 | tf_op jit(solution)/shard_map/while/body/eval_jaxpr/cqhd,ckhd->chqk/dot_general | solution.py:190
  107.5 8.7 %fusion.188 = f32[16,512]{1,0:T(8,128)S(1)} fusion(f32[16,512,512]{2,1,0:T(8,128)} %get-tuple-element.587, f32[16,512]{1,0:T(8,128)S(1)} %bitcast.342), kind=kLoop, calls=%fused_computation.4.clone.1 | loop fusion | flops 12574720 | bytes 16842752 | tf_op jit(solution)/shard_map/while/body/eval_jaxpr/reduce_sum | solution.py:198
  116.2 10.3 %bitcast_add_fusion.8 = f32[1,512,16,64]{1,3,2,0:T(8,128)} fusion(f32[1,512,16,64]{1,3,2,0:T(8,128)} %get-tuple-element.616, bf16[512,16,64]{0,2,1:T(8,128)(2,1)S(1)} %bitcast.337, f32[16,512,512]{2,1,0:T(8,128)} %get-tuple-element.587, f32[16,512]{1,0:T(8,128)S(1)} %bitcast.343, f32[512,16]{0,1:T(8,128)S(1)} %get-tuple-element.589, pred[]{:T(512)S(6)} %compare.27), kind=kOutput, calls=%fused_computation.8.clone.1 | convolution fusion | flops 551026688 | bytes 22085632 | tf_op jit(solution)/shard_map/while/body/eval_jaxpr/chqk,ckhd->cqhd/dot_general | solution.py:199
  129.1 8.2 %bitcast_reduce_fusion.2 = (f32[16,512]{1,0:T(8,128)S(1)}, f32[16,512,512]{2,1,0:T(8,128)}) fusion(bf16[512,16,64]{0,2,1:T(8,128)(2,1)S(1)} %bitcast.339, bf16[1,512,16,64]{1,3,2,0:T(8,128)(2,1)S(1)} %get-tuple-element.629), kind=kOutput, calls=%fused_computation.1.clone.1 | convolution fusion | flops 545251328 | bytes 18907136 | tf_op jit(solution)/shard_map/while/body/eval_jaxpr/cqhd,ckhd->chqk/dot_general | solution.py:190
  137.4 8.7 %fusion.188 = f32[16,512]{1,0:T(8,128)S(1)} fusion(f32[16,512,512]{2,1,0:T(8,128)} %get-tuple-element.587, f32[16,512]{1,0:T(8,128)S(1)} %bitcast.342), kind=kLoop, calls=%fused_computation.4.clone.1 | loop fusion | flops 12574720 | bytes 16842752 | tf_op jit(solution)/shard_map/while/body/eval_jaxpr/reduce_sum | solution.py:198
  146.1 10.9 %bitcast_add_fusion.8 = f32[1,512,16,64]{1,3,2,0:T(8,128)} fusion(f32[1,512,16,64]{1,3,2,0:T(8,128)} %get-tuple-element.616, bf16[512,16,64]{0,2,1:T(8,128)(2,1)S(1)} %bitcast.337, f32[16,512,512]{2,1,0:T(8,128)} %get-tuple-element.587, f32[16,512]{1,0:T(8,128)S(1)} %bitcast.343, f32[512,16]{0,1:T(8,128)S(1)} %get-tuple-element.589, pred[]{:T(512)S(6)} %compare.27), kind=kOutput, calls=%fused_computation.8.clone.1 | convolution fusion | flops 551026688 | bytes 22085632 | tf_op jit(solution)/shard_map/while/body/eval_jaxpr/chqk,ckhd->cqhd/dot_general | solution.py:199
  170.0 21.3 %multiply_convert_fusion.2 = (bf16[512,4096]{1,0:T(8,128)(2,1)}, f32[512,4096]{1,0:T(8,128)}, f32[512,4096]{1,0:T(8,128)}) fusion(bf16[512,16]{0,1:T(8,128)(2,1)S(1)} %convolution_convert_fusion.4, bf16[1,16,4096]{2,0,1:T(2,128)(2,1)S(1)} %fusion.66, f32[512,4096]{1,0:T(8,128)S(1)} %fusion.121, f32[4096]{0:T(1024)S(1)} %copy-done.76), kind=kOutput, calls=%fused_computation.42 | convolution fusion | flops 207618048 | bytes 29523968 | tf_op jit(solution)/shard_map/cra,cae->cre/dot_general | solution.py:94
  191.4 10.5 %add_convert_fusion = bf16[512,4096]{1,0:T(8,128)(2,1)S(1)} fusion(f32[512,4096]{1,0:T(8,128)} %get-tuple-element.441, f32[512,4096]{1,0:T(8,128)} %fusion.62, f32[512,4096]{1,0:T(8,128)} %get-tuple-element.473, bf16[16,512]{1,0:T(8,128)(2,1)S(1)} %copy-done.57, bf16[1,16,4096]{2,0,1:T(2,128)(2,1)S(1)} %copy-done.38), kind=kOutput, calls=%fused_computation.41 | convolution fusion | flops 98566144 | bytes 29507584 | tf_op jit(solution)/shard_map/cra,cad->crd/dot_general | solution.py:103
  201.9 4.5 fusion.123
  223.2 85.0 %while.37 = (s32[]{:T(128)}, f32[1,512,16,64]{1,3,2,0:T(8,128)}, bf16[1,1024,1024]{1,2,0:T(8,128)(2,1)}, bf16[1,1024,1024]{1,2,0:T(8,128)(2,1)}, bf16[1,1024,102...) while((s32[]{:T(128)}, f32[1,512,16,64]{1,3,2,0:T(8,128)}, ...), condition=%wide.region_12.13_spmd.clone, body=%wide.region_11.12_spmd.clone.sunk | while | flops 2720530432 | bytes 139559264 | solution.py:125
  224.7 8.2 %fusion.199 = f32[16,512,512]{2,1,0:T(8,128)} fusion(bf16[512,16,64]{0,2,1:T(8,128)(2,1)S(1)} %bitcast.333, bf16[1,512,16,64]{1,3,2,0:T(8,128)(2,1)S(1)} %get-tuple-element.668), kind=kOutput, calls=%fused_computation.33.clone.1 | convolution fusion | flops 536870912 | bytes 18874368 | tf_op jit(solution)/shard_map/while/body/eval_jaxpr/cqhd,ckhd->chqk/dot_general | solution.py:254
  233.0 10.2 %multiply_convert_fusion.4 = bf16[16,512,512]{2,1,0:T(8,128)(2,1)} fusion(f32[16,512,512]{2,1,0:T(8,128)} %fusion.199, bf16[512,16,64]{0,2,1:T(8,128)(2,1)S(1)} %bitcast.340, f32[16,512]{1,0:T(8,128)S(1)} %bitcast.355, f32[16,512]{1,0:T(8,128)S(1)} %bitcast.350, bf16[1,512,16,64]{1,3,2,0:T(8,128)(2,1)S(1)} %get-tuple-element.671), kind=kOutput, calls=%fused_computation.20.clone.1 | convolution fusion | flops 557842432 | bytes 27328512 | tf_op jit(solution)/shard_map/while/body/eval_jaxpr/cqhd,ckhd->chqk/dot_general | solution.py:258
  243.3 6.2 %bitcast_add_fusion.9 = f32[1,512,16,64]{1,3,2,0:T(8,128)} fusion(f32[1,512,16,64]{1,3,2,0:T(8,128)} %get-tuple-element.650, bf16[512,16,64]{0,2,1:T(8,128)(2,1)S(1)} %bitcast.334, bf16[16,512,512]{2,1,0:T(8,128)(2,1)} %multiply_convert_fusion.4, pred[]{:T(512)S(6)} %compare.28), kind=kOutput, calls=%fused_computation.28.clone.1 | convolution fusion | flops 538443776 | bytes 13631489 | tf_op jit(solution)/shard_map/while/body/eval_jaxpr/chqk,ckhd->cqhd/dot_general | solution.py:273
  249.4 7.5 %fusion.200 = bf16[16,512,64]{1,2,0:T(8,128)(2,1)S(1)} fusion(f32[16,512,512]{2,1,0:T(8,128)} %fusion.199, f32[16,512]{1,0:T(8,128)S(1)} %bitcast.351, bf16[1,512,16,64]{1,3,2,0:T(8,128)(2,1)S(1)} %get-tuple-element.671), kind=kOutput, calls=%fused_computation.23.clone.1 | convolution fusion | flops 549453824 | bytes 18907136 | tf_op jit(solution)/shard_map/while/body/eval_jaxpr/chqk,cqhd->ckhd/dot_general | solution.py:284
  257.0 6.2 %convolution_multiply_fusion.2 = bf16[16,512,64]{1,2,0:T(8,128)(2,1)S(1)} fusion(bf16[16,512,512]{2,1,0:T(8,128)(2,1)} %multiply_convert_fusion.4, bf16[1,512,16,64]{1,3,2,0:T(8,128)(2,1)S(1)} %get-tuple-element.668), kind=kOutput, calls=%fused_computation.29.clone.1 | convolution fusion | flops 537919488 | bytes 10485760 | tf_op jit(solution)/shard_map/while/body/eval_jaxpr/chqk,cqhd->ckhd/dot_general | solution.py:279
  266.8 8.2 %fusion.199 = f32[16,512,512]{2,1,0:T(8,128)} fusion(bf16[512,16,64]{0,2,1:T(8,128)(2,1)S(1)} %bitcast.333, bf16[1,512,16,64]{1,3,2,0:T(8,128)(2,1)S(1)} %get-tuple-element.668), kind=kOutput, calls=%fused_computation.33.clone.1 | convolution fusion | flops 536870912 | bytes 18874368 | tf_op jit(solution)/shard_map/while/body/eval_jaxpr/cqhd,ckhd->chqk/dot_general | solution.py:254
  275.1 10.2 %multiply_convert_fusion.4 = bf16[16,512,512]{2,1,0:T(8,128)(2,1)} fusion(f32[16,512,512]{2,1,0:T(8,128)} %fusion.199, bf16[512,16,64]{0,2,1:T(8,128)(2,1)S(1)} %bitcast.340, f32[16,512]{1,0:T(8,128)S(1)} %bitcast.355, f32[16,512]{1,0:T(8,128)S(1)} %bitcast.350, bf16[1,512,16,64]{1,3,2,0:T(8,128)(2,1)S(1)} %get-tuple-element.671), kind=kOutput, calls=%fused_computation.20.clone.1 | convolution fusion | flops 557842432 | bytes 27328512 | tf_op jit(solution)/shard_map/while/body/eval_jaxpr/cqhd,ckhd->chqk/dot_general | solution.py:258
  285.4 6.8 %bitcast_add_fusion.9 = f32[1,512,16,64]{1,3,2,0:T(8,128)} fusion(f32[1,512,16,64]{1,3,2,0:T(8,128)} %get-tuple-element.650, bf16[512,16,64]{0,2,1:T(8,128)(2,1)S(1)} %bitcast.334, bf16[16,512,512]{2,1,0:T(8,128)(2,1)} %multiply_convert_fusion.4, pred[]{:T(512)S(6)} %compare.28), kind=kOutput, calls=%fused_computation.28.clone.1 | convolution fusion | flops 538443776 | bytes 13631489 | tf_op jit(solution)/shard_map/while/body/eval_jaxpr/chqk,ckhd->cqhd/dot_general | solution.py:273
  292.1 7.5 %fusion.200 = bf16[16,512,64]{1,2,0:T(8,128)(2,1)S(1)} fusion(f32[16,512,512]{2,1,0:T(8,128)} %fusion.199, f32[16,512]{1,0:T(8,128)S(1)} %bitcast.351, bf16[1,512,16,64]{1,3,2,0:T(8,128)(2,1)S(1)} %get-tuple-element.671), kind=kOutput, calls=%fused_computation.23.clone.1 | convolution fusion | flops 549453824 | bytes 18907136 | tf_op jit(solution)/shard_map/while/body/eval_jaxpr/chqk,cqhd->ckhd/dot_general | solution.py:284
  299.7 6.2 %convolution_multiply_fusion.2 = bf16[16,512,64]{1,2,0:T(8,128)(2,1)S(1)} fusion(bf16[16,512,512]{2,1,0:T(8,128)(2,1)} %multiply_convert_fusion.4, bf16[1,512,16,64]{1,3,2,0:T(8,128)(2,1)S(1)} %get-tuple-element.668), kind=kOutput, calls=%fused_computation.29.clone.1 | convolution fusion | flops 537919488 | bytes 10485760 | tf_op jit(solution)/shard_map/while/body/eval_jaxpr/chqk,cqhd->ckhd/dot_general | solution.py:279
  312.7 27.5 %reduce-scatter.4.cloned.1.call-done = bf16[1,512,1024]{1,2,0:T(8,128)(2,1)} async-done(((bf16[1,1024,1024]{1,2,0:T(8,128)(2,1)}), bf16[1,512,1024]{1,2,0:T(8,128)(2,1)}) %reduce-scatter.4.cloned.1.call-update) | async-done | bytes 1048592 | tf_op jit(solution)/shard_map/reduce_scatter | solution.py:307
  342.7 31.6 %reduce-scatter.6.cloned.1.call-done = bf16[1,512,1024]{1,2,0:T(8,128)(2,1)} async-done(((bf16[1,1024,1024]{1,2,0:T(8,128)(2,1)}), bf16[1,512,1024]{1,2,0:T(8,128)(2,1)}) %reduce-scatter.6.cloned.1.call-update) | async-done | bytes 1048592 | tf_op jit(solution)/shard_map/reduce_scatter | solution.py:310
  385.9 54.4 %reduce-scatter.8.cloned.1.call-done = bf16[8,16,8192]{2,1,0:T(8,128)(2,1)} async-done(((bf16[8,16,16384]{2,1,0:T(8,128)(2,1)}), bf16[8,16,8192]{2,1,0:T(8,128)(2,1)}) %reduce-scatter.8.cloned.1.call-update) | async-done | bytes 2097168 | tf_op jit(solution)/shard_map/reduce_scatter | solution.py:335
  440.7 101.3 %all-reduce.2.cloned.1.call-done = bf16[8,16,8192]{2,1,0:T(8,128)(2,1)} async-done(((bf16[8,16,8192]{2,1,0:T(8,128)(2,1)}), bf16[8,16,8192]{2,1,0:T(8,128)(2,1)}) %all-reduce.2.cloned.1.call-update) | async-done | bytes 2097168 | tf_op jit(solution)/shard_map/psum | solution.py:334
  542.1 8.3 %fusion.122 = f32[512,1024]{1,0:T(8,128)S(1)} fusion(bf16[512,4096]{1,0:T(8,128)(2,1)} %get-tuple-element.440, bf16[4096,1024]{1,0:T(8,128)(2,1)} %param.45), kind=kOutput, calls=%fused_computation.231 | convolution fusion | flops 4294967296 | bytes 14680064 | tf_op jit(solution)/shard_map/crd,de->cre/dot_general | solution.py:93
  553.0 6.8 %fusion.110 = f32[512,1024]{1,0:T(8,128)S(1)} fusion(bf16[1024,3072]{1,0:T(8,128)(2,1)} %param.31, bf16[512,1024]{0,1:T(8,128)(2,1)S(1)} %bitcast.368, bf16[512,1024]{0,1:T(8,128)(2,1)S(1)} %bitcast.359, bf16[512,1024]{0,1:T(8,128)(2,1)S(1)} %bitcast.362), kind=kOutput, calls=%fused_computation.223 | convolution fusion | flops 3230662656 | bytes 11534336 | tf_op jit(solution)/shard_map/cre,de->crd/dot_general | solution.py:99
  567.2 32.4 %all-gather.8.cloned.1.call-done = bf16[8,16,16384]{2,1,0:T(8,128)(2,1)} async-done(((bf16[8,16,8192]{2,1,0:T(8,128)(2,1)}), bf16[8,16,16384]{2,1,0:T(8,128)(2,1)}) %all-gather.8.cloned.1.call-update) | async-done | bytes 4194320 | tf_op jit(solution)/shard_map/all_gather | solution.py:336
  (284 shorter events, 117.4 us)
Async XLA Ops:
  7.2 153.3 %copy-start = (bf16[1024,1024]{1,0:T(8,128)(2,1)S(1)}, bf16[1024,1024]{1,0:T(8,128)(2,1)}, u32[]{:S(2)}) copy-start(bf16[1024,1024]{1,0:T(8,128)(2,1)} %param.35) | copy-start | bytes 6291460
  7.2 59.1 %all-gather.6.cloned.1.call-start = ((), (), s32[]{:S(2)}) async-start(), calls=%async_computation.4 | async-start | bytes 3145728 | tf_op jit(solution)/shard_map/all_gather | solution.py:215
  8.8 10.5 %copy-start.61 = (f32[512]{0:T(512)}, f32[512]{0:T(512)S(1)}, u32[]{:S(2)}) copy-start(f32[512]{0:T(512)S(1)} %broadcast_multiply_fusion.5) | copy-start | bytes 6148
  10.5 8.8 %copy-start.63 = (f32[512]{0:T(512)}, f32[512]{0:T(512)S(1)}, u32[]{:S(2)}) copy-start(f32[512]{0:T(512)S(1)} %add_rsqrt_fusion.1) | copy-start | bytes 6148
  25.4 71.2 %all-gather.4.cloned.1.call-start = ((), (), s32[]{:S(2)}) async-start(), calls=%async_computation.3 | async-start | bytes 3145728 | tf_op jit(solution)/shard_map/all_gather | solution.py:214
  36.6 9.3 %copy-start.22 = (bf16[1,512,1024]{2,1,0:T(8,128)(2,1)S(1)}, bf16[1,512,1024]{2,1,0:T(8,128)(2,1)}, u32[]{:S(2)}) copy-start(bf16[1,512,1024]{2,1,0:T(8,128)(2,1)} %param.49) | copy-start | bytes 3145732
  41.9 298.3 %reduce-scatter.4.cloned.1.call-start = ((), (), s32[]{:S(2)}) async-start(), calls=%async_computation.5 | async-start | bytes 3145728 | tf_op jit(solution)/shard_map/reduce_scatter | solution.py:307
  107.5 8.7 %copy-start.3 = (bf16[1,512,1024]{1,2,0:T(8,128)(2,1)S(1)}, bf16[1,512,1024]{1,2,0:T(8,128)(2,1)}, u32[]{:S(2)}) copy-start(bf16[1,512,1024]{1,2,0:T(8,128)(2,1)} %get-tuple-element.588) | copy-start | bytes 3145732 | tf_op jit(solution)/shard_map/while
  137.3 8.7 %copy-start.3 = (bf16[1,512,1024]{1,2,0:T(8,128)(2,1)S(1)}, bf16[1,512,1024]{1,2,0:T(8,128)(2,1)}, u32[]{:S(2)}) copy-start(bf16[1,512,1024]{1,2,0:T(8,128)(2,1)} %get-tuple-element.588) | copy-start | bytes 3145732 | tf_op jit(solution)/shard_map/while
  162.6 45.0 %copy-start.5 = (f32[1,512,1024]{2,1,0:T(8,128)}, f32[1,512,1024]{2,1,0:T(8,128)S(1)}, u32[]{:S(2)}) copy-start(f32[1,512,1024]{2,1,0:T(8,128)S(1)} %get-tuple-element.472) | copy-start | bytes 6291460
  170.0 21.3 %copy-start.38 = (bf16[1,16,4096]{2,0,1:T(2,128)(2,1)S(1)}, bf16[1,16,4096]{2,0,1:T(2,128)(2,1)}, u32[]{:S(2)}) copy-start(bf16[1,16,4096]{2,0,1:T(2,128)(2,1)} %fusion.64) | copy-start | bytes 393220
  170.0 21.3 %copy-start.57 = (bf16[16,512]{1,0:T(8,128)(2,1)S(1)}, bf16[16,512]{1,0:T(8,128)(2,1)}, u32[]{:S(2)}) copy-start(bf16[16,512]{1,0:T(8,128)(2,1)} %convolution_convert_fusion.3) | copy-start | bytes 49156
  224.7 8.2 %copy-start.4 = (bf16[1,1024,1024]{1,2,0:T(8,128)(2,1)S(1)}, bf16[1,1024,1024]{1,2,0:T(8,128)(2,1)}, u32[]{:S(2)}) copy-start(bf16[1,1024,1024]{1,2,0:T(8,128)(2,1)} %get-tuple-element.670) | copy-start | bytes 6291460 | tf_op jit(solution)/shard_map/while
  266.8 8.2 %copy-start.4 = (bf16[1,1024,1024]{1,2,0:T(8,128)(2,1)S(1)}, bf16[1,1024,1024]{1,2,0:T(8,128)(2,1)}, u32[]{:S(2)}) copy-start(bf16[1,1024,1024]{1,2,0:T(8,128)(2,1)} %get-tuple-element.670) | copy-start | bytes 6291460 | tf_op jit(solution)/shard_map/while
  308.2 66.0 %reduce-scatter.6.cloned.1.call-start = ((), (), s32[]{:S(2)}) async-start(), calls=%async_computation.6 | async-start | bytes 3145728 | tf_op jit(solution)/shard_map/reduce_scatter | solution.py:310
  308.8 32.9 %copy-start.2 = (f32[1,512,16,64]{1,3,2,0:T(8,128)S(1)}, f32[1,512,16,64]{1,3,2,0:T(8,128)}, u32[]{:S(2)}) copy-start(f32[1,512,16,64]{1,3,2,0:T(8,128)} %get-tuple-element.310) | copy-start | bytes 6291460
  308.8 32.9 %copy-start.35 = (f32[512,32]{0,1:T(8,128)S(1)}, f32[512,32]{0,1:T(8,128)}, u32[]{:S(2)}) copy-start(f32[512,32]{0,1:T(8,128)} %copy-done.34) | copy-start | bytes 196612
  308.8 32.9 %copy-start.37 = (f32[512,32]{0,1:T(8,128)S(1)}, f32[512,32]{0,1:T(8,128)}, u32[]{:S(2)}) copy-start(f32[512,32]{0,1:T(8,128)} %copy-done.36) | copy-start | bytes 196612
  308.9 131.5 %reduce-scatter.8.cloned.1.call-start = ((), (), s32[]{:S(2)}) async-start(), calls=%async_computation.8 | async-start | bytes 6291456 | tf_op jit(solution)/shard_map/reduce_scatter | solution.py:335
  341.8 32.5 %copy-start.41 = (bf16[1,16,3072]{2,0,1:T(2,128)(2,1)S(1)}, bf16[1,16,3072]{2,0,1:T(2,128)(2,1)}, u32[]{:S(2)}) copy-start(bf16[1,16,3072]{2,0,1:T(2,128)(2,1)} %copy-done.40) | copy-start | bytes 294916
  342.5 33.6 %copy-start.29 = (bf16[1,512,16,64]{1,3,2,0:T(8,128)(2,1)}, bf16[1,512,16,64]{1,3,2,0:T(8,128)(2,1)S(1)}, u32[]{:S(2)}) copy-start(bf16[1,512,16,64]{1,3,2,0:T(8,128)(2,1)S(1)} %pad_maximum_fusion.4) | copy-start | bytes 3145732
  342.6 33.5 %copy-start.31 = (bf16[1,512,16,64]{1,3,2,0:T(8,128)(2,1)}, bf16[1,512,16,64]{1,3,2,0:T(8,128)(2,1)S(1)}, u32[]{:S(2)}) copy-start(bf16[1,512,16,64]{1,3,2,0:T(8,128)(2,1)S(1)} %pad_maximum_fusion.3) | copy-start | bytes 3145732
  342.6 33.5 %copy-start.12 = (bf16[1,512,1024]{2,1,0:T(8,128)(2,1)S(1)}, bf16[1,512,1024]{2,1,0:T(8,128)(2,1)}, u32[]{:S(2)}) copy-start(bf16[1,512,1024]{2,1,0:T(8,128)(2,1)} %param.27) | copy-start | bytes 3145732
  342.6 33.5 %copy-start.62 = (f32[512]{0:T(512)S(1)}, f32[512]{0:T(512)}, u32[]{:S(2)}) copy-start(f32[512]{0:T(512)} %copy-done.61) | copy-start | bytes 6148
  342.6 33.5 %copy-start.64 = (f32[512]{0:T(512)S(1)}, f32[512]{0:T(512)}, u32[]{:S(2)}) copy-start(f32[512]{0:T(512)} %copy-done.63) | copy-start | bytes 6148
  342.7 33.5 %copy-start.71 = (f32[1024]{0:T(1024)S(1)}, f32[1024]{0:T(1024)}, u32[]{:S(2)}) copy-start(f32[1024]{0:T(1024)} %param.29) | copy-start | bytes 12292
  342.7 33.5 %copy-start.78 = (f32[1024]{0:T(1024)S(1)}, f32[1024]{0:T(1024)}, u32[]{:S(2)}) copy-start(f32[1024]{0:T(1024)} %param.30) | copy-start | bytes 12292
  385.9 156.1 %all-reduce.2.cloned.1.call-start = ((), (), s32[]{:S(2)}) async-start(), calls=%async_computation.9 | async-start | bytes 4194304 | tf_op jit(solution)/shard_map/psum | solution.py:334
  440.4 159.2 %all-gather.8.cloned.1.call-start = ((), (), s32[]{:S(2)}) async-start(), calls=%async_computation.7 | async-start | bytes 6291456 | tf_op jit(solution)/shard_map/all_gather | solution.py:336
  542.0 8.3 %copy-start.6 = (f32[1,512,1024]{2,1,0:T(8,128)S(1)}, f32[1,512,1024]{2,1,0:T(8,128)}, u32[]{:S(2)}) copy-start(f32[1,512,1024]{2,1,0:T(8,128)} %copy-done.5) | copy-start | bytes 6291460
  542.0 8.3 %copy-start.45 = (bf16[1,16,1024]{2,0,1:T(2,128)(2,1)S(1)}, bf16[1,16,1024]{2,0,1:T(2,128)(2,1)}, u32[]{:S(2)}) copy-start(bf16[1,16,1024]{2,0,1:T(2,128)(2,1)} %copy-done.44) | copy-start | bytes 98308
  542.1 8.3 %copy-start.73 = (f32[1024]{0:T(1024)S(1)}, f32[1024]{0:T(1024)}, u32[]{:S(2)}) copy-start(f32[1024]{0:T(1024)} %param.46) | copy-start | bytes 12292
  (62 other events, 227.8 us)
Sparse Core Ops, SparseCore 0:
  25.5 35.8 all-gather.5
  63.5 33.1 all-gather.3
  308.4 31.8 reduce-scatter.3
  342.4 31.8 reduce-scatter.5
  386.0 54.2 reduce-scatter.7
  444.2 97.8 all-reduce.1
  543.6 55.9 all-gather.7
where the time goes:
time: 622 us; the launch traced here: 614 us
  waiting for transfers between devices  274 us (44%)
  matrix products  227 us (36%)
  other arithmetic  47.6 us (8%)
  local copies, waits for them, and re-layouts  46.8 us (8%)
  between operations  16.4 us (3%)
    psum x1, waiting for transfers between devices, body(): summed = lax.psum(packed.astype(jnp.bfloat16), 'dp')  101 us
    reduce_scatter x1, waiting for transfers between devices, body(): lax.psum_scatter(summed, 'seq', scatter_dimension=2, tiled=True)  54.4 us
    all_gather x1, waiting for transfers between devices, body(): lax.all_gather(owned.astype(jnp.bfloat16), 'seq', axis=2, tiled=True)  32.4 us
    reduce_scatter x1, waiting for transfers between devices, body(): lax.psum_scatter(value_full.astype(jnp.bfloat16), 'seq', scatter_dimensio...  31.6 us
    reduce_scatter x1, waiting for transfers between devices, body(): lax.psum_scatter(key_full.astype(jnp.bfloat16), 'seq', scatter_dimension=...  27.5 us
    all_gather x1, waiting for transfers between devices, body(): lax.all_gather(key_low, 'seq', axis=1, tiled=True)  26.5 us
    dot_general x4, matrix products, project(): jnp.einsum('cra,cae->cre', low_rank, up_pick, preferred_element_type=jnp....  24.4 us
    dot_general x4, matrix products, project_back(): jnp.einsum('cre,de->crd', grad_low, weight, preferred_element_type=jnp.fl...  23 us
  transfers between devices with their start and end apart: 7, of which 6 were waited for; matrix products, arithmetic and copies ran while one was open for 12% of the time, Pallas kernels for 0%

commit v1 on v0

--- a/solution.py
+++ b/solution.py
@@ -331,7 +331,9 @@
     packed = jnp.einsum(
         "ca,crw->arw", onehot.astype(jnp.float32), packed_clip, precision=lax.Precision.HIGHEST
     )
-    summed = lax.psum(packed.astype(jnp.bfloat16), "dp")
+    part = packed.astype(jnp.bfloat16)
+    parts = lax.all_gather(part, "dp")
+    summed = jnp.sum(parts, axis=0)
     owned = lax.psum_scatter(summed, "seq", scatter_dimension=2, tiled=True).astype(jnp.float32)
     gathered = lax.all_gather(owned.astype(jnp.bfloat16), "seq", axis=2, tiled=True).astype(
         owned.dtype

time: 622 us -> 858 us (1.38)
  waiting for transfers between devices: 274 us -> 500 us
  other arithmetic: 47.6 us -> 71.1 us
  matrix products: 227 us -> 209 us
    all_gather x0 -> x1, waiting for transfers between devices: none -> 326 us  [body(): parts = lax.all_gather(part, 'dp')]
    psum x1 -> x0, waiting for transfers between devices: 101 us -> none  [body(): summed = lax.psum(packed.astype(jnp.bfloat16), 'dp')]
    reduce_sum x0 -> x1, other arithmetic: none -> 23.7 us  [body(): summed = jnp.sum(parts, axis=0)]
    dot_general x2, matrix products: 12.9 us -> 3 us  [backward_step(): jnp.einsum('chqk,ckhd->cqhd', grad_score, key_heads, preferred_element_ty...]
  transfers between devices with their start and end apart: 7 -> 7, of which waited for: 6 -> 6; matrix products, arithmetic and copies ran while one was open for 12% -> 9% of each run, Pallas kernels for 0% -> 0%
where the time goes in v1:
time: 858 us; the launch traced here: 849 us
  waiting for transfers between devices  500 us (58%)
  matrix products  209 us (24%)
  other arithmetic  71.1 us (8%)
  local copies, waits for them, and re-layouts  51 us (6%)
  between operations  16.5 us (2%)
    all_gather x1, waiting for transfers between devices, body(): parts = lax.all_gather(part, 'dp')  326 us
    reduce_scatter x1, waiting for transfers between devices, body(): lax.psum_scatter(summed, 'seq', scatter_dimension=2, tiled=True)  54.1 us
    all_gather x1, waiting for transfers between devices, body(): lax.all_gather(owned.astype(jnp.bfloat16), 'seq', axis=2, tiled=True)  33.2 us
    reduce_scatter x1, waiting for transfers between devices, body(): lax.psum_scatter(value_full.astype(jnp.bfloat16), 'seq', scatter_dimensio...  31.6 us
    reduce_scatter x1, waiting for transfers between devices, body(): lax.psum_scatter(key_full.astype(jnp.bfloat16), 'seq', scatter_dimension=...  27.5 us
    all_gather x1, waiting for transfers between devices, body(): lax.all_gather(key_low, 'seq', axis=1, tiled=True)  26.4 us
    dot_general x4, matrix products, project(): jnp.einsum('cra,cae->cre', low_rank, up_pick, preferred_element_type=jnp....  24.5 us
    reduce_sum x1, other arithmetic, body(): summed = jnp.sum(parts, axis=0)  23.7 us
  transfers between devices with their start and end apart: 7, of which 6 were waited for; matrix products, arithmetic and copies ran while one was open for 9% of the time, Pallas kernels for 0%

profile of v1, /device:TPU:0, one launch (start us, length us, event | category | flops | bytes accessed | tf_op | source)
XLA Modules:
  0.0 848.8 jit_solution(4285656545800320498)
XLA Ops:
  14.9 5.8 fusion.113
  26.3 4.8 fusion.116
  37.5 4.2 subtract_convert_fusion.2
  56.8 10.4 %fusion.62 = f32[512,4096]{1,0:T(8,128)} fusion(bf16[4096,1024]{1,0:T(8,128)(2,1)} %param.45, bf16[1,512,1024]{2,1,0:T(8,128)(2,1)S(1)} %copy-done.24), kind=kOutput, calls=%fused_computation.125 | convolution fusion | flops 4294967296 | bytes 17825792 | tf_op jit(solution)/shard_map/cre,de->crd/dot_general | solution.py:99
  67.1 3.9 copy.51
  71.1 26.4 %all-gather.6.cloned.1.call-done = bf16[1,1024,1024]{1,2,0:T(8,128)(2,1)} async-done(((bf16[1,512,1024]{1,2,0:T(8,128)(2,1)}), bf16[1,1024,1024]{1,2,0:T(8,128)(2,1)}) %all-gather.6.cloned.1.call-update) | async-done | bytes 2097168 | tf_op jit(solution)/shard_map/all_gather | solution.py:214
  97.5 58.6 %while.36 = (s32[]{:T(128)}, f32[1,16,512]{2,1,0:T(8,128)S(1)}, f32[1,16,512]{2,1,0:T(8,128)S(1)}, f32[1,512,16,64]{1,3,2,0:T(8,128)}, bf16[1,1024,1024]{1,2,0:T...) while((s32[]{:T(128)}, f32[1,16,512]{2,1,0:T(8,128)S(1)}, ...), condition=%wide.region_5.6_spmd.clone, body=%wide.region_2.5_spmd.clone.sunk | while | flops 1108918272 | bytes 62390448 | solution.py:125
  99.2 8.2 bitcast_reduce_fusion.2
  107.4 8.6 %fusion.188 = f32[16,512]{1,0:T(8,128)S(1)} fusion(f32[16,512,512]{2,1,0:T(8,128)} %get-tuple-element.604, f32[16,512]{1,0:T(8,128)S(1)} %bitcast.343), kind=kLoop, calls=%fused_computation.4.clone.1 | loop fusion | flops 12574720 | bytes 16842752 | tf_op jit(solution)/shard_map/while/body/eval_jaxpr/reduce_sum | solution.py:198
  116.0 10.3 %bitcast_add_fusion.8 = f32[1,512,16,64]{1,3,2,0:T(8,128)} fusion(f32[1,512,16,64]{1,3,2,0:T(8,128)} %get-tuple-element.633, bf16[512,16,64]{0,2,1:T(8,128)(2,1)S(1)} %bitcast.338, f32[16,512,512]{2,1,0:T(8,128)} %get-tuple-element.604, f32[16,512]{1,0:T(8,128)S(1)} %bitcast.344, f32[512,16]{0,1:T(8,128)S(1)} %get-tuple-element.606, pred[]{:T(512)S(6)} %compare.27), kind=kOutput, calls=%fused_computation.8.clone.1 | convolution fusion | flops 551026688 | bytes 22085632 | tf_op jit(solution)/shard_map/while/body/eval_jaxpr/chqk,ckhd->cqhd/dot_general | solution.py:199
  128.0 8.2 bitcast_reduce_fusion.2
  136.2 8.6 %fusion.188 = f32[16,512]{1,0:T(8,128)S(1)} fusion(f32[16,512,512]{2,1,0:T(8,128)} %get-tuple-element.604, f32[16,512]{1,0:T(8,128)S(1)} %bitcast.343), kind=kLoop, calls=%fused_computation.4.clone.1 | loop fusion | flops 12574720 | bytes 16842752 | tf_op jit(solution)/shard_map/while/body/eval_jaxpr/reduce_sum | solution.py:198
  144.8 10.9 %bitcast_add_fusion.8 = f32[1,512,16,64]{1,3,2,0:T(8,128)} fusion(f32[1,512,16,64]{1,3,2,0:T(8,128)} %get-tuple-element.633, bf16[512,16,64]{0,2,1:T(8,128)(2,1)S(1)} %bitcast.338, f32[16,512,512]{2,1,0:T(8,128)} %get-tuple-element.604, f32[16,512]{1,0:T(8,128)S(1)} %bitcast.344, f32[512,16]{0,1:T(8,128)S(1)} %get-tuple-element.606, pred[]{:T(512)S(6)} %compare.27), kind=kOutput, calls=%fused_computation.8.clone.1 | convolution fusion | flops 551026688 | bytes 22085632 | tf_op jit(solution)/shard_map/while/body/eval_jaxpr/chqk,ckhd->cqhd/dot_general | solution.py:199
  164.2 4.5 fusion.121
  168.8 21.4 %multiply_convert_fusion.2 = (bf16[512,4096]{1,0:T(8,128)(2,1)}, f32[512,4096]{1,0:T(8,128)}, f32[512,4096]{1,0:T(8,128)}) fusion(bf16[512,16]{0,1:T(8,128)(2,1)S(1)} %convolution_convert_fusion.4, bf16[1,16,4096]{2,0,1:T(2,128)(2,1)S(1)} %fusion.66, f32[512,4096]{1,0:T(8,128)S(1)} %fusion.121, f32[4096]{0:T(1024)S(1)} %copy-done.75), kind=kOutput, calls=%fused_computation.42 | convolution fusion | flops 207618048 | bytes 29523968 | tf_op jit(solution)/shard_map/cra,cae->cre/dot_general | solution.py:94
  190.2 10.5 %add_convert_fusion = bf16[512,4096]{1,0:T(8,128)(2,1)S(1)} fusion(f32[512,4096]{1,0:T(8,128)} %get-tuple-element.458, f32[512,4096]{1,0:T(8,128)} %fusion.62, f32[512,4096]{1,0:T(8,128)} %get-tuple-element.490, bf16[16,512]{1,0:T(8,128)(2,1)S(1)} %copy-done.56, bf16[1,16,4096]{2,0,1:T(2,128)(2,1)S(1)} %copy-done.37), kind=kOutput, calls=%fused_computation.41 | convolution fusion | flops 98566144 | bytes 29507584 | tf_op jit(solution)/shard_map/cra,cad->crd/dot_general | solution.py:103
  201.9 4.5 fusion.123
  221.6 71.3 %while.37 = (s32[]{:T(128)}, f32[1,512,16,64]{1,3,2,0:T(8,128)}, bf16[1,1024,1024]{1,2,0:T(8,128)(2,1)}, bf16[1,1024,1024]{1,2,0:T(8,128)(2,1)}, bf16[1,1024,102...) while((s32[]{:T(128)}, f32[1,512,16,64]{1,3,2,0:T(8,128)}, ...), condition=%wide.region_12.13_spmd.clone, body=%wide.region_11.12_spmd.clone.sunk | while | flops 2720530432 | bytes 135364960 | solution.py:125
  225.3 8.2 fusion.199
  233.5 8.5 %fusion.200 = bf16[16,512,64]{1,2,0:T(8,128)(2,1)} fusion(f32[16,512,512]{2,1,0:T(8,128)} %fusion.199, f32[16,512]{1,0:T(8,128)S(1)} %bitcast.351, bf16[1,512,16,64]{1,3,2,0:T(8,128)(2,1)S(1)} %get-tuple-element.688), kind=kOutput, calls=%fused_computation.23.clone.1 | convolution fusion | flops 549453824 | bytes 18907136 | tf_op jit(solution)/shard_map/while/body/eval_jaxpr/chqk,cqhd->ckhd/dot_general | solution.py:284
  242.0 8.5 %multiply_convert_fusion.4 = bf16[16,512,512]{2,1,0:T(8,128)(2,1)S(1)} fusion(f32[16,512,512]{2,1,0:T(8,128)} %fusion.199, bf16[512,16,64]{0,2,1:T(8,128)(2,1)} %bitcast.341, f32[16,512]{1,0:T(8,128)S(1)} %bitcast.356, f32[16,512]{1,0:T(8,128)S(1)} %bitcast.352, bf16[1,512,16,64]{1,3,2,0:T(8,128)(2,1)S(1)} %get-tuple-element.688), kind=kOutput, calls=%fused_computation.20.clone.1 | convolution fusion | flops 557842432 | bytes 27328512 | tf_op jit(solution)/shard_map/while/body/eval_jaxpr/cqhd,ckhd->chqk/dot_general | solution.py:258
  260.9 8.2 fusion.199
  269.0 8.5 %fusion.200 = bf16[16,512,64]{1,2,0:T(8,128)(2,1)} fusion(f32[16,512,512]{2,1,0:T(8,128)} %fusion.199, f32[16,512]{1,0:T(8,128)S(1)} %bitcast.351, bf16[1,512,16,64]{1,3,2,0:T(8,128)(2,1)S(1)} %get-tuple-element.688), kind=kOutput, calls=%fused_computation.23.clone.1 | convolution fusion | flops 549453824 | bytes 18907136 | tf_op jit(solution)/shard_map/while/body/eval_jaxpr/chqk,cqhd->ckhd/dot_general | solution.py:284
  277.5 8.5 %multiply_convert_fusion.4 = bf16[16,512,512]{2,1,0:T(8,128)(2,1)S(1)} fusion(f32[16,512,512]{2,1,0:T(8,128)} %fusion.199, bf16[512,16,64]{0,2,1:T(8,128)(2,1)} %bitcast.341, f32[16,512]{1,0:T(8,128)S(1)} %bitcast.356, f32[16,512]{1,0:T(8,128)S(1)} %bitcast.352, bf16[1,512,16,64]{1,3,2,0:T(8,128)(2,1)S(1)} %get-tuple-element.688), kind=kOutput, calls=%fused_computation.20.clone.1 | convolution fusion | flops 557842432 | bytes 27328512 | tf_op jit(solution)/shard_map/while/body/eval_jaxpr/cqhd,ckhd->chqk/dot_general | solution.py:258
  297.4 27.5 %reduce-scatter.4.cloned.1.call-done = bf16[1,512,1024]{1,2,0:T(8,128)(2,1)} async-done(((bf16[1,1024,1024]{1,2,0:T(8,128)(2,1)}), bf16[1,512,1024]{1,2,0:T(8,128)(2,1)}) %reduce-scatter.4.cloned.1.call-update) | async-done | bytes 1048592 | tf_op jit(solution)/shard_map/reduce_scatter | solution.py:307
  327.3 31.6 %reduce-scatter.6.cloned.1.call-done = bf16[1,512,1024]{1,2,0:T(8,128)(2,1)} async-done(((bf16[1,1024,1024]{1,2,0:T(8,128)(2,1)}), bf16[1,512,1024]{1,2,0:T(8,128)(2,1)}) %reduce-scatter.6.cloned.1.call-update) | async-done | bytes 1048592 | tf_op jit(solution)/shard_map/reduce_scatter | solution.py:310
  370.6 326.2 %all-gather.12.cloned.1.call-done = bf16[128,16,16384]{2,1,0:T(8,128)(2,1)} async-done(((bf16[8,16,16384]{2,1,0:T(8,128)(2,1)}), bf16[128,16,16384]{2,1,0:T(8,128)(2,1)}) %all-gather.12.cloned.1.call-update) | async-done | bytes 67108880 | tf_op jit(solution)/shard_map/all_gather | solution.py:335
  696.8 23.7 %reduce_sum.118 = bf16[8,16,16384]{2,1,0:T(8,128)(2,1)} reduce(bf16[16,8,16,16384]{3,2,1,0:T(8,128)(2,1)} %bitcast.52, bf16[]{:T(256)} %constant.235.clone.1), dimensions={0}, to_apply=%region_17.18 | reduce | flops 31457280 | bytes 71303168 | tf_op jit(solution)/shard_map/reduce_sum | solution.py:336
  720.9 54.1 %reduce-scatter.8.cloned.1.call-done = bf16[8,16,8192]{2,1,0:T(8,128)(2,1)} async-done(((bf16[8,16,16384]{2,1,0:T(8,128)(2,1)}), bf16[8,16,8192]{2,1,0:T(8,128)(2,1)}) %reduce-scatter.8.cloned.1.call-update) | async-done | bytes 2097168 | tf_op jit(solution)/shard_map/reduce_scatter | solution.py:337
  775.0 8.3 fusion.122
  786.1 6.8 fusion.110
  800.2 33.2 %all-gather.10.cloned.1.call-done = bf16[8,16,16384]{2,1,0:T(8,128)(2,1)} async-done(((bf16[8,16,8192]{2,1,0:T(8,128)(2,1)}), bf16[8,16,16384]{2,1,0:T(8,128)(2,1)}) %all-gather.10.cloned.1.call-update) | async-done | bytes 4194320 | tf_op jit(solution)/shard_map/all_gather | solution.py:338
  (281 shorter events, 118.5 us)
Async XLA Ops:
  7.2 152.1 %copy-start = (bf16[1024,1024]{1,0:T(8,128)(2,1)S(1)}, bf16[1024,1024]{1,0:T(8,128)(2,1)}, u32[]{:S(2)}) copy-start(bf16[1024,1024]{1,0:T(8,128)(2,1)} %param.35) | copy-start | bytes 6291460
  7.2 7.7 copy-start.11
  7.2 7.7 copy-start.69
  7.2 59.9 %all-gather.8.cloned.1.call-start = ((), (), s32[]{:S(2)}) async-start(), calls=%async_computation.4 | async-start | bytes 3145728 | tf_op jit(solution)/shard_map/all_gather | solution.py:215
  9.6 11.2 %copy-start.60 = (f32[512]{0:T(512)}, f32[512]{0:T(512)S(1)}, u32[]{:S(2)}) copy-start(f32[512]{0:T(512)S(1)} %broadcast_multiply_fusion.5) | copy-start | bytes 6148
  11.2 9.6 %copy-start.62 = (f32[512]{0:T(512)}, f32[512]{0:T(512)S(1)}, u32[]{:S(2)}) copy-start(f32[512]{0:T(512)S(1)} %add_rsqrt_fusion.1) | copy-start | bytes 6148
  26.3 71.2 %all-gather.6.cloned.1.call-start = ((), (), s32[]{:S(2)}) async-start(), calls=%async_computation.3 | async-start | bytes 3145728 | tf_op jit(solution)/shard_map/all_gather | solution.py:214
  37.5 9.3 %copy-start.23 = (bf16[1,512,1024]{2,1,0:T(8,128)(2,1)S(1)}, bf16[1,512,1024]{2,1,0:T(8,128)(2,1)}, u32[]{:S(2)}) copy-start(bf16[1,512,1024]{2,1,0:T(8,128)(2,1)} %param.49) | copy-start | bytes 3145732
  42.8 282.1 %reduce-scatter.4.cloned.1.call-start = ((), (), s32[]{:S(2)}) async-start(), calls=%async_computation.5 | async-start | bytes 3145728 | tf_op jit(solution)/shard_map/reduce_scatter | solution.py:307
  161.3 45.1 %copy-start.6 = (f32[1,512,1024]{2,1,0:T(8,128)}, f32[1,512,1024]{2,1,0:T(8,128)S(1)}, u32[]{:S(2)}) copy-start(f32[1,512,1024]{2,1,0:T(8,128)S(1)} %get-tuple-element.489) | copy-start | bytes 6291460
  168.8 21.4 %copy-start.37 = (bf16[1,16,4096]{2,0,1:T(2,128)(2,1)S(1)}, bf16[1,16,4096]{2,0,1:T(2,128)(2,1)}, u32[]{:S(2)}) copy-start(bf16[1,16,4096]{2,0,1:T(2,128)(2,1)} %fusion.64) | copy-start | bytes 393220
  168.8 21.4 %copy-start.56 = (bf16[16,512]{1,0:T(8,128)(2,1)S(1)}, bf16[16,512]{1,0:T(8,128)(2,1)}, u32[]{:S(2)}) copy-start(bf16[16,512]{1,0:T(8,128)(2,1)} %convolution_convert_fusion.3) | copy-start | bytes 49156
  242.0 8.5 %copy-start.2 = (f32[1,512,16,64]{1,3,2,0:T(8,128)S(1)}, f32[1,512,16,64]{1,3,2,0:T(8,128)}, u32[]{:S(2)}) copy-start(f32[1,512,16,64]{1,3,2,0:T(8,128)} %get-tuple-element.667) | copy-start | bytes 6291460 | tf_op jit(solution)/shard_map/while
  277.5 8.5 %copy-start.2 = (f32[1,512,16,64]{1,3,2,0:T(8,128)S(1)}, f32[1,512,16,64]{1,3,2,0:T(8,128)}, u32[]{:S(2)}) copy-start(f32[1,512,16,64]{1,3,2,0:T(8,128)} %get-tuple-element.667) | copy-start | bytes 6291460 | tf_op jit(solution)/shard_map/while
  292.9 66.0 %reduce-scatter.6.cloned.1.call-start = ((), (), s32[]{:S(2)}) async-start(), calls=%async_computation.6 | async-start | bytes 3145728 | tf_op jit(solution)/shard_map/reduce_scatter | solution.py:310
  293.5 32.9 %copy-start.4 = (f32[1,512,16,64]{1,3,2,0:T(8,128)S(1)}, f32[1,512,16,64]{1,3,2,0:T(8,128)}, u32[]{:S(2)}) copy-start(f32[1,512,16,64]{1,3,2,0:T(8,128)} %get-tuple-element.310) | copy-start | bytes 6291460
  293.5 32.9 %copy-start.34 = (f32[512,32]{0,1:T(8,128)S(1)}, f32[512,32]{0,1:T(8,128)}, u32[]{:S(2)}) copy-start(f32[512,32]{0,1:T(8,128)} %copy-done.33) | copy-start | bytes 196612
  293.5 32.9 %copy-start.36 = (f32[512,32]{0,1:T(8,128)S(1)}, f32[512,32]{0,1:T(8,128)}, u32[]{:S(2)}) copy-start(f32[512,32]{0,1:T(8,128)} %copy-done.35) | copy-start | bytes 196612
  293.5 403.3 %all-gather.12.cloned.1.call-start = ((), (), s32[]{:S(2)}) async-start(), calls=%async_computation.9 | async-start | bytes 71303168 | tf_op jit(solution)/shard_map/all_gather | solution.py:335
  326.4 32.5 %copy-start.40 = (bf16[1,16,3072]{2,0,1:T(2,128)(2,1)S(1)}, bf16[1,16,3072]{2,0,1:T(2,128)(2,1)}, u32[]{:S(2)}) copy-start(bf16[1,16,3072]{2,0,1:T(2,128)(2,1)} %copy-done.39) | copy-start | bytes 294916
  327.2 33.6 %copy-start.28 = (bf16[1,512,16,64]{1,3,2,0:T(8,128)(2,1)}, bf16[1,512,16,64]{1,3,2,0:T(8,128)(2,1)S(1)}, u32[]{:S(2)}) copy-start(bf16[1,512,16,64]{1,3,2,0:T(8,128)(2,1)S(1)} %pad_maximum_fusion.3) | copy-start | bytes 3145732
  327.2 33.5 %copy-start.30 = (bf16[1,512,16,64]{1,3,2,0:T(8,128)(2,1)}, bf16[1,512,16,64]{1,3,2,0:T(8,128)(2,1)S(1)}, u32[]{:S(2)}) copy-start(bf16[1,512,16,64]{1,3,2,0:T(8,128)(2,1)S(1)} %pad_maximum_fusion.4) | copy-start | bytes 3145732
  327.3 33.5 %copy-start.13 = (bf16[1,512,1024]{2,1,0:T(8,128)(2,1)S(1)}, bf16[1,512,1024]{2,1,0:T(8,128)(2,1)}, u32[]{:S(2)}) copy-start(bf16[1,512,1024]{2,1,0:T(8,128)(2,1)} %param.27) | copy-start | bytes 3145732
  327.3 33.5 %copy-start.61 = (f32[512]{0:T(512)S(1)}, f32[512]{0:T(512)}, u32[]{:S(2)}) copy-start(f32[512]{0:T(512)} %copy-done.60) | copy-start | bytes 6148
  327.3 33.5 %copy-start.63 = (f32[512]{0:T(512)S(1)}, f32[512]{0:T(512)}, u32[]{:S(2)}) copy-start(f32[512]{0:T(512)} %copy-done.62) | copy-start | bytes 6148
  327.3 33.5 %copy-start.70 = (f32[1024]{0:T(1024)S(1)}, f32[1024]{0:T(1024)}, u32[]{:S(2)}) copy-start(f32[1024]{0:T(1024)} %param.29) | copy-start | bytes 12292
  327.3 33.5 %copy-start.77 = (f32[1024]{0:T(1024)S(1)}, f32[1024]{0:T(1024)}, u32[]{:S(2)}) copy-start(f32[1024]{0:T(1024)} %param.30) | copy-start | bytes 12292
  370.6 404.4 %reduce-scatter.8.cloned.1.call-start = ((), (), s32[]{:S(2)}) async-start(), calls=%async_computation.7 | async-start | bytes 6291456 | tf_op jit(solution)/shard_map/reduce_scatter | solution.py:337
  720.5 112.8 %all-gather.10.cloned.1.call-start = ((), (), s32[]{:S(2)}) async-start(), calls=%async_computation.8 | async-start | bytes 6291456 | tf_op jit(solution)/shard_map/all_gather | solution.py:338
  775.0 8.3 copy-start.7
  775.0 8.3 copy-start.44
  775.0 8.3 copy-start.72
  (60 other events, 205.7 us)
Sparse Core Ops, SparseCore 0:
  26.4 35.7 all-gather.7
  64.4 33.1 all-gather.5
  293.0 31.8 reduce-scatter.3
  327.0 31.8 reduce-scatter.5
  370.7 326.1 all-gather.11
  720.7 54.2 reduce-scatter.7
  776.6 56.7 all-gather.9
